TPU v7x, 32 devices: a whole 2x2x4 slice. The times are simulated.
32 devices in a mesh: groups: 2 (over x), tok: 16 (over z, y, core).
Axes of the slice: x: 2, y: 2, z: 4, core: 2. Of those that a mesh axis runs over, the one named last changes fastest.
Arguments:
- queries: bfloat16 [16384, 2048], P(('groups', 'tok')), parts along dimension 0, may hold values from -6 to 6
- keys: bfloat16 [16384, 2048], P(('groups', 'tok')), parts along dimension 0, may hold values from -6 to 6
- values: bfloat16 [16384, 2048], P(('groups', 'tok')), parts along dimension 0, may hold values from -6 to 6
- rates: float32 [16384, 4], P(('groups', 'tok')), parts along dimension 0, may hold values from 0.00024414062 to 0.001953125
- split_row: int32 [32], P(('groups', 'tok')), parts along dimension 0, may hold values from 128 to 384, as said below
- fast_init: float32 [512, 3072], P('tok'), may hold values from -0.25 to 0.25
Outputs:
- mixed: bfloat16 [16384, 2048], P(('groups', 'tok')), parts along dimension 0
There are 2 independent parts, one for each index of `groups`. A program takes and returns all parts, laid end to end along the dimension named above; an argument that names none is the same for every part. Nothing has to cross between parts.
Inputs may be any that keep to these rules, and one draw needn't show every extreme that they name: `split_row`: some index of tok has exactly 128 and some exactly 384.
All inputs are finite; a program needn't handle non-finite values.
Results may differ from a plain program's by a relative error of at most 0.012.
The roundings to bfloat16 on the way count: a program that leaves them out, or rounds other values in their place, can miss the bound.
Values may be sent and summed in bfloat16 or wider, within the bound.
A program may use at most 128 MiB of HBM per device.

v0:
```python
import jax
import jax.numpy as jnp
from jax import lax
from jax.sharding import PartitionSpec as P

MOMENTUM_DECAY = 0.9
EPSILON = 1e-06


def gather_weights(shard, heads, hidden):
    gathered = lax.all_gather(shard, "tok", axis=0, tiled=True)
    return gathered.reshape(gathered.shape[0], 3, heads, hidden)


def products(stacked, gathered):
    gates = jnp.einsum("rhj,jhf->rhf", stacked, gathered[:, 0], preferred_element_type=jnp.float32)
    ups = jnp.einsum("rhj,jhf->rhf", stacked, gathered[:, 1], preferred_element_type=jnp.float32)
    return (gates, ups)


def segment_gradient(key_heads, value_heads, rates, keep, gates, ups, down, owned_rows):
    sigma = jax.nn.sigmoid(gates)
    active = gates * sigma
    hidden_act = (active * ups).astype(jnp.bfloat16)
    scale = -(rates * keep[:, None].astype(jnp.float32))
    outer_grad = (scale[:, :, None] * value_heads.astype(jnp.float32)).astype(jnp.bfloat16)
    hidden_grad = jnp.einsum("rhj,jhf->rhf", outer_grad, down, preferred_element_type=jnp.float32)
    backward_gate_grad = (hidden_grad * ups * sigma * (1.0 + gates * (1.0 - sigma))).astype(
        jnp.bfloat16
    )
    backward_up_grad = (hidden_grad * active).astype(jnp.bfloat16)
    grad_gate = jnp.einsum(
        "rhj,rhf->jhf", key_heads, backward_gate_grad, preferred_element_type=jnp.float32
    )
    grad_up = jnp.einsum(
        "rhj,rhf->jhf", key_heads, backward_up_grad, preferred_element_type=jnp.float32
    )
    grad_gate, grad_up = (grad_gate, grad_up)
    grad_down = jnp.einsum(
        "rhj,rhf->jhf", outer_grad, hidden_act, preferred_element_type=jnp.float32
    )
    return lax.psum_scatter(
        jnp.stack([grad_gate, grad_up, grad_down], axis=1).reshape(
            lax.axis_size("tok") * owned_rows, -1
        ),
        "tok",
        scatter_dimension=0,
        tiled=True,
    )


def owner_update(state, momentum, gradient, initial, heads, hidden):
    momentum = MOMENTUM_DECAY * momentum + gradient
    moved = (state - momentum).reshape(state.shape[0], 3 * heads, hidden)
    base = initial.reshape(state.shape[0], 3 * heads, hidden)
    target = jnp.sqrt(jnp.mean(base * base, axis=-1, keepdims=True))
    current = jnp.sqrt(jnp.mean(moved * moved, axis=-1, keepdims=True) + EPSILON)
    return ((moved * (target / current)).reshape(state.shape), momentum)


def apply_fast(gates, ups, down):
    query_hidden = (jax.nn.silu(gates) * ups).astype(jnp.bfloat16)
    return jnp.einsum("rhf,jhf->rhj", query_hidden, down, preferred_element_type=jnp.float32)


def per_device(queries, keys, values, rates, split_row, fast_init):
    token_rows = queries.shape[0]
    heads = rates.shape[1]
    width = queries.shape[1] // heads
    hidden = fast_init.shape[1] // (3 * heads)
    owned_rows = fast_init.shape[0]
    query_heads = queries.reshape(token_rows, heads, width)
    key_heads = keys.reshape(token_rows, heads, width)
    value_heads = values.reshape(token_rows, heads, width)
    first = jnp.arange(token_rows) < split_row[0]
    second = jnp.logical_not(first)
    momentum = jnp.zeros_like(fast_init)
    gathered = gather_weights(fast_init.astype(jnp.bfloat16), heads, hidden)
    gates, ups = products(key_heads, gathered)
    gradient = segment_gradient(
        key_heads, value_heads, rates, first, gates, ups, gathered[:, 2], owned_rows
    )
    state, momentum = owner_update(fast_init, momentum, gradient, fast_init, heads, hidden)
    gathered = gather_weights(state.astype(jnp.bfloat16), heads, hidden)
    down = gathered[:, 2]
    stacked = jnp.concatenate([query_heads, key_heads], axis=0)
    gates, ups = products(stacked, gathered)
    out_first = apply_fast(gates[:token_rows], ups[:token_rows], down)
    gradient = segment_gradient(
        key_heads,
        value_heads,
        rates,
        second,
        gates[token_rows:],
        ups[token_rows:],
        down,
        owned_rows,
    )
    state, momentum = owner_update(state, momentum, gradient, fast_init, heads, hidden)
    gathered = gather_weights(state.astype(jnp.bfloat16), heads, hidden)
    gates, ups = products(query_heads, gathered)
    out_second = apply_fast(gates, ups, gathered[:, 2])
    mixed = jnp.where(first[:, None, None], out_first, out_second)
    return mixed.astype(jnp.bfloat16).reshape(token_rows, heads * width)


def solution(mesh):
    in_specs = (
        P(("groups", "tok"), None),
        P(("groups", "tok"), None),
        P(("groups", "tok"), None),
        P(("groups", "tok"), None),
        P(("groups", "tok")),
        P("tok", None),
    )
    out_specs = P(("groups", "tok"), None)
    return jax.shard_map(
        per_device, mesh=mesh, in_specs=in_specs, out_specs=out_specs, check_vma=False
    )
```

profile of v0, /device:TPU:1, one launch (start us, length us, event | category | flops | bytes accessed | tf_op | source)
XLA Modules:
  0.0 399.7 jit_solution(14757153980645999825)
XLA Ops:
  6.5 1.7 convert_element_type.72
  8.2 0.0 all-gather.4.cloned.1.call-update
  8.3 0.0 reduce-scatter.3.cloned.1.call-start
  9.0 2.9 copy.67
  11.8 4.0 %convert_element_type.87 = f32[512,2048]{1,0:T(8,128)} convert(bf16[512,2048]{1,0:T(8,128)(2,1)} %param.8) | non-fusion elementwise | flops 1048576 | bytes 6291456 | tf_op jit(solution)/shard_map/convert_element_type | solution.py:26
  15.9 0.6 multiply_negate_fusion
  16.5 40.9 %all-gather.4.cloned.1.call-done = bf16[512,3072]{1,0:T(8,128)(2,1)} async-done(((bf16[32,3072]{1,0:T(8,128)(2,1)}), bf16[512,3072]{1,0:T(8,128)(2,1)}) %all-gather.4.cloned.1.call-update) | async-done | bytes 3145744 | tf_op jit(solution)/shard_map/all_gather | solution.py:11
  57.4 4.7 %copy.65 = bf16[512,3072]{0,1:T(8,128)(2,1)} copy(bf16[512,3072]{1,0:T(8,128)(2,1)} %all-gather.4.cloned.1.call-done) | data formatting | bytes 6291456 | tf_op jit(solution)/shard_map/all_gather | solution.py:11
  62.1 2.3 fusion.31
  64.3 0.9 fusion.32
  65.2 1.3 copy-done
  66.5 1.0 fusion.33
  67.6 1.4 convolution_bitcast_fusion.3
  69.0 1.4 convolution_bitcast_fusion.5
  70.4 1.2 convolution_bitcast_fusion.4
  71.6 3.3 pad_maximum_fusion
  74.9 6.6 %copy.77 = f32[512,3072]{1,0:T(8,128)} copy(f32[512,3072]{0,1:T(8,128)} %bitcast.185) | data formatting | bytes 12582912 | tf_op jit(solution)/shard_map/reshape | solution.py:43
  81.5 0.0 reduce-scatter.3.cloned.1.call-update
  81.5 0.0 all-gather.6.cloned.1.call-start
  81.6 83.0 %reduce-scatter.3.cloned.1.call-done = f32[32,3072]{1,0:T(8,128)} async-done(((f32[512,3072]{1,0:T(8,128)}), f32[32,3072]{1,0:T(8,128)}) %reduce-scatter.3.cloned.1.call-update) | async-done | bytes 393232 | tf_op jit(solution)/shard_map/reduce_scatter | solution.py:42
  164.6 1.8 fusion.58
  166.4 0.1 mul.148
  166.6 0.1 mul.146
  166.7 0.0 copy-start.10
  166.7 0.1 reduce_sum.32
  166.8 0.1 reduce_sum.27
  167.0 0.1 mul.149
  167.1 0.2 copy.125
  167.4 0.3 copy-done.10
  167.7 0.7 fusion.57
  168.4 0.0 all-gather.6.cloned.1.call-update
  168.4 0.2 reduce-scatter.5.cloned.1.call-start
  168.7 2.4 copy.81
  171.0 3.9 copy.79
  175.0 4.2 %copy.80 = bf16[512,4,512]{2,0,1:T(8,128)(2,1)} copy(bf16[512,4,512]{0,2,1:T(8,128)(2,1)} %bitcast.187) | data formatting | bytes 4194304 | tf_op jit(solution)/shard_map/reshape | solution.py:72
  179.1 35.1 %all-gather.6.cloned.1.call-done = bf16[512,3072]{1,0:T(8,128)(2,1)} async-done(((bf16[32,3072]{1,0:T(8,128)(2,1)}), bf16[512,3072]{1,0:T(8,128)(2,1)}) %all-gather.6.cloned.1.call-update) | async-done | bytes 3145744 | tf_op jit(solution)/shard_map/all_gather | solution.py:11
  214.2 4.7 %copy.78 = bf16[512,3072]{0,1:T(8,128)(2,1)} copy(bf16[512,3072]{1,0:T(8,128)(2,1)} %all-gather.6.cloned.1.call-done) | data formatting | bytes 6291456 | tf_op jit(solution)/shard_map/all_gather | solution.py:11
  219.0 4.0 fusion.4
  223.0 0.1 copy-done.6
  223.1 0.6 copy-done.7
  223.7 1.5 fusion.5
  225.2 3.6 copy-done.1
  228.8 1.0 fusion.38
  229.8 1.5 convolution_bitcast_fusion
  231.3 1.3 convolution_bitcast_fusion.2
  232.7 1.1 convolution_bitcast_fusion.1
  233.8 3.3 pad_maximum_fusion.1
  237.1 6.6 %copy.92 = f32[512,3072]{1,0:T(8,128)} copy(f32[512,3072]{0,1:T(8,128)} %bitcast.186) | data formatting | bytes 12582912 | tf_op jit(solution)/shard_map/reshape | solution.py:43
  243.7 0.0 reduce-scatter.5.cloned.1.call-update
  243.7 0.3 all-gather.8.cloned.1.call-start
  244.0 82.8 %reduce-scatter.5.cloned.1.call-done = f32[32,3072]{1,0:T(8,128)} async-done(((f32[512,3072]{1,0:T(8,128)}), f32[32,3072]{1,0:T(8,128)}) %reduce-scatter.5.cloned.1.call-update) | async-done | bytes 393232 | tf_op jit(solution)/shard_map/reduce_scatter | solution.py:42
  326.8 1.1 fusion.56
  327.9 0.1 mul.168
  328.1 0.1 reduce_sum.33
  328.2 0.1 mul.169
  328.4 0.2 copy.126
  328.6 0.7 multiply_convert_fusion.2
  329.4 0.0 all-gather.8.cloned.1.call-update
  329.4 5.0 %fusion.28 = bf16[4,512,512]{2,1,0:T(8,128)(2,1)} fusion(f32[1024,4,256]{2,0,1:T(8,128)} %copy-done.14, f32[1024,4,256]{2,0,1:T(8,128)} %copy-done.13, bf16[512,3,4,256]{0,3,2,1:T(8,128)(2,1)} %bitcast.196), kind=kOutput, calls=%fused_computation.51 | convolution fusion | flops 540016640 | bytes 7340032 | tf_op jit(solution)/shard_map/rhf,jhf->rhj/dot_general | solution.py:63
  334.4 40.7 %all-gather.8.cloned.1.call-done = bf16[512,3072]{1,0:T(8,128)(2,1)} async-done(((bf16[32,3072]{1,0:T(8,128)(2,1)}), bf16[512,3072]{1,0:T(8,128)(2,1)}) %all-gather.8.cloned.1.call-update) | async-done | bytes 3145744 | tf_op jit(solution)/shard_map/all_gather | solution.py:11
  375.1 4.7 %copy.93 = bf16[512,3072]{0,1:T(8,128)(2,1)} copy(bf16[512,3072]{1,0:T(8,128)(2,1)} %all-gather.8.cloned.1.call-done) | data formatting | bytes 6291456 | tf_op jit(solution)/shard_map/all_gather | solution.py:11
  379.8 3.5 fusion.30
  383.3 6.0 %select_convert_fusion = bf16[4,512,512]{2,1,0:T(8,128)(2,1)} fusion(bf16[4,512,512]{2,1,0:T(8,128)(2,1)} %fusion.28, pred[512]{0:T(512)(128)(4,1)S(1)} %iota_compare_fusion, f32[4,256,512]{1,2,0:T(8,128)} %fusion.30, bf16[512,4,512]{0,2,1:T(8,128)(2,1)S(1)} %bitcast.189, bf16[512,3,4,256]{0,3,2,1:T(8,128)(2,1)} %bitcast.194), kind=kOutput, calls=%fused_computation.7 | convolution fusion | flops 1077936128 | bytes 10486272 | tf_op jit(solution)/shard_map/rhf,jhf->rhj/dot_general | solution.py:63
  389.3 3.9 copy.99
  (29 shorter events, 0.1 us)
Async XLA Ops:
  6.5 50.8 %all-gather.4.cloned.1.call-start = ((), (), s32[]{:S(2)}) async-start(), calls=%async_computation.2 | async-start | bytes 3342336 | tf_op jit(solution)/shard_map/all_gather | solution.py:11
  8.3 156.3 %reduce-scatter.3.cloned.1.call-start = ((), (), s32[]{:S(2)}) async-start(), calls=%async_computation.3 | async-start | bytes 6684672 | tf_op jit(solution)/shard_map/reduce_scatter | solution.py:42
  11.8 4.1 %copy-start.12 = (f32[512,4]{0,1:T(4,128)S(1)}, f32[512,4]{0,1:T(4,128)}, u32[]{:S(2)}) copy-start(f32[512,4]{0,1:T(4,128)} %param.9) | copy-start | bytes 24580
  62.0 2.3 copy-start.3
  64.3 2.2 copy-start
  81.5 83.1 %copy-start.9 = (f32[32,3072]{1,0:T(8,128)S(1)}, f32[32,3072]{1,0:T(8,128)}, u32[]{:S(2)}) copy-start(f32[32,3072]{1,0:T(8,128)} %param.11) | copy-start | bytes 1179652
  81.5 132.7 %all-gather.6.cloned.1.call-start = ((), (), s32[]{:S(2)}) async-start(), calls=%async_computation.4 | async-start | bytes 3342336 | tf_op jit(solution)/shard_map/all_gather | solution.py:11
  166.7 1.0 copy-start.10
  168.4 158.4 %reduce-scatter.5.cloned.1.call-start = ((), (), s32[]{:S(2)}) async-start(), calls=%async_computation.5 | async-start | bytes 6684672 | tf_op jit(solution)/shard_map/reduce_scatter | solution.py:42
  219.0 4.0 copy-start.4
  219.0 4.1 %copy-start.6 = (bf16[512,4,512]{2,0,1:T(8,128)(2,1)S(1)}, bf16[512,4,512]{2,0,1:T(8,128)(2,1)}, u32[]{:S(2)}) copy-start(bf16[512,4,512]{2,0,1:T(8,128)(2,1)} %copy.81) | copy-start | bytes 6291460
  219.0 4.7 %copy-start.7 = (bf16[512,4,512]{2,0,1:T(8,128)(2,1)S(1)}, bf16[512,4,512]{2,0,1:T(8,128)(2,1)}, u32[]{:S(2)}) copy-start(bf16[512,4,512]{2,0,1:T(8,128)(2,1)} %copy.80) | copy-start | bytes 6291460
  223.7 9.0 %copy-start.13 = (f32[1024,4,256]{2,0,1:T(8,128)}, f32[1024,4,256]{2,0,1:T(8,128)S(1)}, u32[]{:S(2)}) copy-start(f32[1024,4,256]{2,0,1:T(8,128)S(1)} %fusion.4) | copy-start | bytes 12582916
  223.7 5.1 %copy-start.1 = (f32[512,2048]{1,0:T(8,128)S(1)}, f32[512,2048]{1,0:T(8,128)}, u32[]{:S(2)}) copy-start(f32[512,2048]{1,0:T(8,128)} %convert_element_type.87) | copy-start | bytes 12582916
  223.7 5.1 %copy-start.11 = (f32[512,4]{0,1:T(4,128)S(1)}, f32[512,4]{0,1:T(4,128)}, u32[]{:S(2)}) copy-start(f32[512,4]{0,1:T(4,128)} %get-tuple-element.10) | copy-start | bytes 24580
  225.2 6.1 %copy-start.14 = (f32[1024,4,256]{2,0,1:T(8,128)}, f32[1024,4,256]{2,0,1:T(8,128)S(1)}, u32[]{:S(2)}) copy-start(f32[1024,4,256]{2,0,1:T(8,128)S(1)} %fusion.5) | copy-start | bytes 12582916
  243.7 83.1 %copy-start.5 = (f32[32,3072]{1,0:T(8,128)S(1)}, f32[32,3072]{1,0:T(8,128)}, u32[]{:S(2)}) copy-start(f32[32,3072]{1,0:T(8,128)} %reduce-scatter.3.cloned.1.call-done) | copy-start | bytes 1179652
  243.7 131.4 %all-gather.8.cloned.1.call-start = ((), (), s32[]{:S(2)}) async-start(), calls=%async_computation.6 | async-start | bytes 3342336 | tf_op jit(solution)/shard_map/all_gather | solution.py:11
  326.8 1.8 copy-start.8
  334.4 45.4 %copy-start.2 = (bf16[512,2048]{0,1:T(8,128)(2,1)S(1)}, bf16[512,2048]{0,1:T(8,128)(2,1)}, u32[]{:S(2)}) copy-start(bf16[512,2048]{0,1:T(8,128)(2,1)} %copy.79) | copy-start | bytes 6291460
Sparse Core Ops, SparseCore 0:
  9.6 47.6 all-gather.3
  81.6 82.9 reduce-scatter.2
  168.6 45.6 all-gather.5
  243.9 82.8 reduce-scatter.4
  329.5 45.5 all-gather.7
where the time goes:
time: 401 us; the launch traced here: 400 us
  waiting for transfers between devices  283 us (71%)
  local copies, waits for them, and re-layouts  51.5 us (13%)
  matrix products  33 us (8%)
  other arithmetic  17.9 us (4%)
  between operations  14.1 us (4%)
    reduce_scatter x2, waiting for transfers between devices, segment_gradient(): lax.psum_scatter(jnp.stack([grad_gate, grad_up, grad_down], axis=1).resha...  166 us
    all_gather x3, waiting for transfers between devices, gather_weights(): gathered = lax.all_gather(shard, 'tok', axis=0, tiled=True)  117 us
    all_gather x3, local copies, waits for them, and re-layouts, gather_weights(): gathered = lax.all_gather(shard, 'tok', axis=0, tiled=True)  14.1 us
    unnamed x34, local copies, waits for them, and re-layouts  13.2 us
    reshape x2, local copies, waits for them, and re-layouts, segment_gradient(): jnp.stack([grad_gate, grad_up, grad_down], axis=1)  13.2 us
    dot_general x2, matrix products, apply_fast(): jnp.einsum('rhf,jhf->rhj', query_hidden, down, preferred_element_type=jnp...  11 us
    dot_general x3, matrix products, products(): jnp.einsum('rhj,jhf->rhf', stacked, gathered[:, 0], preferred_element_typ...  9.69 us
  transfers between devices with their start and end apart: 5, of which 5 were waited for; matrix products, arithmetic and copies ran while one was open for 6% of the time, Pallas kernels for 0%

commit v1 on v0

--- a/solution.py
+++ b/solution.py
@@ -1,10 +1,303 @@
+import functools
+
 import jax
 import jax.numpy as jnp
 from jax import lax
+from jax.experimental import pallas as pl
+from jax.experimental.pallas import tpu as pltpu
 from jax.sharding import PartitionSpec as P
 
 MOMENTUM_DECAY = 0.9
 EPSILON = 1e-06
+MESH = pl.DeviceIdType.MESH
+BF16 = jnp.bfloat16
+F32 = jnp.float32
+NY, NC = 2, 2
+
+
+def dot(lhs, rhs, lhs_dim, rhs_dim):
+    return lax.dot_general(
+        lhs, rhs, (((lhs_dim,), (rhs_dim,)), ((), ())), preferred_element_type=F32
+    )
+
+
+def step_kernel(
+    dims,
+    q_hbm, k_hbm, v_hbm, rates_ref, split_ref, init_ref, out_ref,
+    q_ref, k_ref, v_ref, w, grad, half, core_in, quarter, y_in, z_in, state, momentum,
+    load_sem, agz_s, agz_r, agy_s, agy_r, agc_s, agc_r,
+    rsc_s, rsc_r, rsy_s, rsy_r, rsz_s, rsz_r,
+):
+    heads, rows, width, hidden, nz, owned = dims
+    me = lax.axis_index("tok")
+    c0 = lax.rem(me, NC)
+    y0 = lax.rem(me // NC, NY)
+    z0 = me // (NC * NY)
+    c1, y1 = 1 - c0, 1 - y0
+    z_peers = [lax.rem(z0 + i, nz) for i in range(1, nz)]
+    trimmed = rows - rows // 4
+
+    def device(z, y, c):
+        return {"tok": (z * NY + y) * NC + c}
+
+    partner, y_peer = device(z0, y0, c1), device(z0, y1, c0)
+
+    def remote(src, dst, send_sem, recv_sem, target):
+        return pltpu.make_async_remote_copy(
+            src_ref=src, dst_ref=dst, send_sem=send_sem, recv_sem=recv_sem,
+            device_id=target, device_id_type=MESH,
+        )
+
+    loads = [
+        pltpu.make_async_copy(src, dst, load_sem.at[i])
+        for i, (src, dst) in enumerate(((k_hbm, k_ref), (v_hbm, v_ref), (q_hbm, q_ref)))
+    ]
+
+    def ag_z_copies(r, h):
+        mine = w.at[r, h, z0, y0, c0]
+        return [
+            remote(mine, mine, agz_s.at[r, h, i], agz_r.at[r, h, z0], device(zp, y0, c0))
+            for i, zp in enumerate(z_peers)
+        ]
+
+    def ag_y_copy(r, h):
+        mine = w.at[r, h, :, y0, c0]
+        return remote(mine, mine, agy_s.at[r, h], agy_r.at[r, h], y_peer)
+
+    def ag_c_copy(r, h):
+        mine = w.at[r, h, :, :, c0]
+        return remote(mine, mine, agc_s.at[r, h], agc_r.at[r, h], partner)
+
+    def rs_c_copy(r, h):
+        return remote(
+            grad.at[r, h, :, :, c1], core_in.at[r, h], rsc_s.at[r, h], rsc_r.at[r, h], partner
+        )
+
+    def rs_y_copy(r, h):
+        return remote(
+            half.at[r, h, :, y1], y_in.at[r, h], rsy_s.at[r, h], rsy_r.at[r, h], y_peer
+        )
+
+    def rs_z_copies(r, h):
+        return [
+            remote(
+                quarter.at[r, h, zp], z_in.at[r, h, z0], rsz_s.at[r, h, i], rsz_r.at[r, h, z0],
+                device(zp, y0, c0),
+            )
+            for i, zp in enumerate(z_peers)
+        ]
+
+    def ag_z(r, h):
+        for copy in ag_z_copies(r, h):
+            copy.start()
+
+    def ag_y(r, h):
+        for i, zp in enumerate(z_peers):
+            there = w.at[r, h, zp, y0, c0]
+            remote(there, there, agz_s.at[r, h, i], agz_r.at[r, h, zp], y_peer).wait_recv()
+        ag_y_copy(r, h).start()
+
+    def ag_c(r, h):
+        there = w.at[r, h, :, y1, c0]
+        remote(there, there, agy_s.at[r, h], agy_r.at[r, h], y_peer).wait_recv()
+        ag_c_copy(r, h).start()
+
+    def gathered(r, h):
+        return w[r, h].reshape(width, 3 * hidden)
+
+    def head_columns(h):
+        return pl.ds(pl.multiple_of(h * width, width), width)
+
+    def gradient(r, h):
+        there = w.at[r, h, :, :, c1]
+        remote(there, there, agc_s.at[r, h], agc_r.at[r, h], partner).wait_recv()
+        low = 0 if r == 0 else rows - trimmed
+        weights = gathered(r, h)
+        keys = k_ref[low : low + trimmed, head_columns(h)]
+        values = v_ref[low : low + trimmed, head_columns(h)]
+        row = low + lax.broadcasted_iota(jnp.int32, (trimmed, 1), 0)
+        first = row < split_ref[0]
+        keep = first if r == 0 else jnp.logical_not(first)
+        all_rates = rates_ref[low : low + trimmed, :]
+        lane = lax.broadcasted_iota(jnp.int32, all_rates.shape, 1)
+        rate = jnp.sum(jnp.where(lane == h, all_rates, 0.0), axis=1, keepdims=True)
+        scale = -(rate * keep.astype(F32))
+        dout = (scale * values.astype(F32)).astype(BF16)
+        both = dot(keys, weights[:, : 2 * hidden], 1, 0)
+        dhid = dot(dout, weights[:, 2 * hidden :], 1, 0)
+        gates, ups = both[:, :hidden], both[:, hidden:]
+        sigma = jax.nn.sigmoid(gates)
+        active = gates * sigma
+        hid = (active * ups).astype(BF16)
+        dg = (dhid * ups * sigma * (1.0 + gates * (1.0 - sigma))).astype(BF16)
+        du = (dhid * active).astype(BF16)
+        to_both = dot(keys, jnp.concatenate([dg, du], axis=1), 0, 0)
+        to_down = dot(dout, hid, 0, 0)
+        grad[r, h, :, :, :, :, : 2 * hidden] = to_both.astype(BF16).reshape(
+            nz, NY, NC, owned, 2 * hidden
+        )
+        grad[r, h, :, :, :, :, 2 * hidden :] = to_down.astype(BF16).reshape(
+            nz, NY, NC, owned, hidden
+        )
+        rs_c_copy(r, h).start()
+
+    def rs_y(r, h):
+        rs_c_copy(r, h).wait_recv()
+        half[r, h] = (grad[r, h, :, :, c0].astype(F32) + core_in[r, h].astype(F32)).astype(BF16)
+        rs_y_copy(r, h).start()
+
+    def rs_z(r, h):
+        rs_y_copy(r, h).wait_recv()
+        quarter[r, h] = (half[r, h, :, y0].astype(F32) + y_in[r, h].astype(F32)).astype(BF16)
+        for copy in rs_z_copies(r, h):
+            copy.start()
+
+    def initial(m, h):
+        return init_ref[:, pl.ds(pl.multiple_of((m * heads + h) * hidden, hidden), hidden)]
+
+    def update(r, h):
+        total = quarter[r, h, z0].astype(F32)
+        for i, zp in enumerate(z_peers):
+            there = z_in.at[r, h, zp]
+            remote(there, there, rsz_s.at[r, h, i], rsz_r.at[r, h, zp], y_peer).wait_recv()
+            total = total + z_in[r, h, zp].astype(F32)
+        for m in range(3):
+            part = slice(m * hidden, (m + 1) * hidden)
+            base = initial(m, h)
+            if r == 0:
+                moment = total[:, part]
+                moved = base - moment
+                momentum[h, :, part] = moment
+            else:
+                moved = state[h, :, part] - (MOMENTUM_DECAY * momentum[h, :, part] + total[:, part])
+            target = jnp.sqrt(jnp.mean(base * base, axis=-1, keepdims=True))
+            current = jnp.sqrt(jnp.mean(moved * moved, axis=-1, keepdims=True) + EPSILON)
+            new = moved * (target / current)
+            if r == 0:
+                state[h, :, part] = new
+            w[r + 1, h, z0, y0, c0, :, part] = new.astype(BF16)
+        ag_z(r + 1, h)
+
+    def apply(r, h):
+        low = 0 if r == 1 else rows - trimmed
+        weights = gathered(r, h)
+        queries = q_ref[low : low + trimmed, head_columns(h)]
+        both = dot(queries, weights[:, : 2 * hidden], 1, 0)
+        gates, ups = both[:, :hidden], both[:, hidden:]
+        hid = (gates * jax.nn.sigmoid(gates) * ups).astype(BF16)
+        return dot(hid, weights[:, 2 * hidden :], 1, 1).astype(BF16)
+
+    def apply_first(h):
+        out_ref[:trimmed, head_columns(h)] = apply(1, h)
+
+    def apply_second(h):
+        there = w.at[2, h, :, :, c1]
+        remote(there, there, agc_s.at[2, h], agc_r.at[2, h], partner).wait_recv()
+        second = apply(2, h)
+        low = rows - trimmed
+        row = low + lax.broadcasted_iota(jnp.int32, (trimmed - low, 1), 0)
+        out_ref[low:trimmed, head_columns(h)] = jnp.where(
+            row < split_ref[0],
+            out_ref[low:trimmed, head_columns(h)].astype(F32),
+            second[: trimmed - low].astype(F32),
+        ).astype(BF16)
+        out_ref[trimmed:, head_columns(h)] = second[trimmed - low :]
+
+    for load in loads:
+        load.start()
+    barrier = pltpu.get_barrier_semaphore()
+    peers = [partner, y_peer] + [device(zp, y0, c0) for zp in z_peers]
+    for peer in peers:
+        pl.semaphore_signal(barrier, inc=1, device_id=peer, device_id_type=MESH)
+    for h in range(heads):
+        for m in range(3):
+            w[0, h, z0, y0, c0, :, m * hidden : (m + 1) * hidden] = initial(m, h).astype(BF16)
+    pl.semaphore_wait(barrier, len(peers))
+    for h in range(heads):
+        ag_z(0, h)
+    for load in loads:
+        load.wait()
+
+    stages = []
+    for r in range(2):
+        stages += [
+            functools.partial(stage, r) for stage in (ag_y, ag_c, gradient, rs_y, rs_z, update)
+        ]
+    stages += [functools.partial(ag_y, 2), functools.partial(ag_c, 2), apply_second]
+    order = [(s, stages[s]) for s in reversed(range(len(stages)))] + [(9, apply_first)]
+
+    def tick(t, carry):
+        for s, stage in order:
+            h = t - s
+
+            @pl.when(jnp.logical_and(h >= 0, h < heads))
+            def _():
+                stage(h)
+
+        return carry
+
+    lax.fori_loop(0, len(stages) + heads - 1, tick, 0)
+
+    def drain(h, carry):
+        for r in range(3):
+            for copy in ag_z_copies(r, h) + [ag_y_copy(r, h), ag_c_copy(r, h)]:
+                copy.wait_send()
+        for r in range(2):
+            for copy in [rs_c_copy(r, h), rs_y_copy(r, h)] + rs_z_copies(r, h):
+                copy.wait_send()
+        return carry
+
+    lax.fori_loop(0, heads, drain, 0)
+
+
+def fused_step(queries, keys, values, rates, split_row, fast_init):
+    rows, features = queries.shape
+    heads = rates.shape[1]
+    width = features // heads
+    hidden = fast_init.shape[1] // (3 * heads)
+    owned = fast_init.shape[0]
+    nz = lax.axis_size("tok") // (NY * NC)
+    chunk = (owned, 3 * hidden)
+    hbm = pl.BlockSpec(memory_space=pl.ANY)
+    vmem = pl.BlockSpec(memory_space=pltpu.VMEM)
+    dma = pltpu.SemaphoreType.DMA
+    return pl.pallas_call(
+        functools.partial(step_kernel, (heads, rows, width, hidden, nz, owned)),
+        out_shape=jax.ShapeDtypeStruct((rows, features), BF16),
+        in_specs=[hbm, hbm, hbm, vmem, pl.BlockSpec(memory_space=pltpu.SMEM), vmem],
+        out_specs=vmem,
+        scratch_shapes=[
+            pltpu.VMEM((rows, features), BF16),
+            pltpu.VMEM((rows, features), BF16),
+            pltpu.VMEM((rows, features), BF16),
+            pltpu.VMEM((3, heads, nz, NY, NC) + chunk, BF16),
+            pltpu.VMEM((2, heads, nz, NY, NC) + chunk, BF16),
+            pltpu.VMEM((2, heads, nz, NY) + chunk, BF16),
+            pltpu.VMEM((2, heads, nz, NY) + chunk, BF16),
+            pltpu.VMEM((2, heads, nz) + chunk, BF16),
+            pltpu.VMEM((2, heads, nz) + chunk, BF16),
+            pltpu.VMEM((2, heads, nz) + chunk, BF16),
+            pltpu.VMEM((heads,) + chunk, F32),
+            pltpu.VMEM((heads,) + chunk, F32),
+            dma((3,)),
+            dma((3, heads, nz - 1)),
+            dma((3, heads, nz)),
+            dma((3, heads)),
+            dma((3, heads)),
+            dma((3, heads)),
+            dma((3, heads)),
+            dma((2, heads)),
+            dma((2, heads)),
+            dma((2, heads)),
+            dma((2, heads)),
+            dma((2, heads, nz - 1)),
+            dma((2, heads, nz)),
+        ],
+        compiler_params=pltpu.CompilerParams(
+            collective_id=0, has_side_effects=True, vmem_limit_bytes=60 * 1024 * 1024
+        ),
+        name="fast_weight_step",
+    )(queries, keys, values, rates, split_row, fast_init)
 
 
 def gather_weights(shard, heads, hidden):
@@ -104,6 +397,14 @@
     return mixed.astype(jnp.bfloat16).reshape(token_rows, heads * width)
 
 
+def plan(*args):
+    size = lax.axis_size("tok")
+    small = size // (NY * NC) in (2, 3, 4) and size % (NY * NC) == 0
+    if small and args[5].shape[0] % 16 == 0:
+        return fused_step(*args)
+    return per_device(*args)
+
+
 def solution(mesh):
     in_specs = (
         P(("groups", "tok"), None),
@@ -115,5 +416,5 @@
     )
     out_specs = P(("groups", "tok"), None)
     return jax.shard_map(
-        per_device, mesh=mesh, in_specs=in_specs, out_specs=out_specs, check_vma=False
-    )
+        plan, mesh=mesh, in_specs=in_specs, out_specs=out_specs, check_vma=False
+    )

time: 401 us -> 135 us (0.34)
  waiting for transfers between devices: 283 us -> 0 us
  Pallas kernels: 0 us -> 130 us
  local copies, waits for them, and re-layouts: 51.5 us -> 4.71 us
  matrix products: 33 us -> 0 us
  other arithmetic: 17.9 us -> 0 us
  between operations: 14.1 us -> 0.66 us
    reduce_scatter x2 -> x0, waiting for transfers between devices: 166 us -> none  [segment_gradient(): lax.psum_scatter(jnp.stack([grad_gate, grad_up, grad_down], axis=1).resha...]
    pallas_call x0 -> x1, Pallas kernels: none -> 130 us  [fused_step(): pl.pallas_call(functools.partial(step_kernel, (heads, rows, width, hidden...]
    all_gather x3 -> x0, waiting for transfers between devices: 117 us -> none  [gather_weights(): gathered = lax.all_gather(shard, 'tok', axis=0, tiled=True)]
    dot_general x15 -> x0, matrix products: 33 us -> none  [the longest x2 11 us: apply_fast(): jnp.einsum('rhf,jhf->rhj', query_hidden, down, preferred_element_type=jnp...]
    reshape x5 -> x0, local copies, waits for them, and re-layouts: 23.6 us -> none  [the longest x2 13.2 us: segment_gradient(): jnp.stack([grad_gate, grad_up, grad_down], axis=1)]
    all_gather x3 -> x0, local copies, waits for them, and re-layouts: 14.1 us -> none  [gather_weights(): gathered = lax.all_gather(shard, 'tok', axis=0, tiled=True)]
    unnamed x34 -> x2, local copies, waits for them, and re-layouts: 13.2 us -> 4.71 us
    convert_element_type x5 -> x0, other arithmetic: 7.23 us -> none  [the longest x1 4.04 us: segment_gradient(): value_heads.astype(jnp.float32)]
  transfers between devices with their start and end apart: 5 -> 0, of which waited for: 5 -> 0; matrix products, arithmetic and copies ran while one was open for 6% -> 0% of each run, Pallas kernels for 0% -> 0%
where the time goes in v1:
time: 135 us
  Pallas kernels  130 us (96%)
  local copies, waits for them, and re-layouts  4.71 us (3%)
    pallas_call x1, Pallas kernels, fused_step(): pl.pallas_call(functools.partial(step_kernel, (heads, rows, width, hidden...  130 us
    unnamed x2, local copies, waits for them, and re-layouts  4.71 us

profile of v1, /device:TPU:1, one launch (start us, length us, event | category | flops | bytes accessed | tf_op | source)
XLA Modules:
  0.0 135.2 jit_solution(15329608672945249643)
XLA Ops:
  0.7 1.6 %copy.7.rates_ref = f32[512,4]{1,0:T(8,128)} copy(f32[512,4]{0,1:T(4,128)} %param.9) | data formatting | bytes 16384 | tf_op args[3]
  2.2 129.8 %fast_weight_step.1 = bf16[512,2048]{1,0:T(8,128)(2,1)} custom-call(bf16[512,2048]{1,0:T(8,128)(2,1)} %q_hbm.1, bf16[512,2048]{1,0:T(8,128)(2,1)} %k_hbm.1, bf16[512,2048]{1,0:T(8,128)(2,1)} %v_hbm.1, f32[512,4]{1,0:T(8,128)} %copy.7.rates_ref, s32[1]{0:T(128)S(6)} %copy.9.split_ref, f32[32,3072]{1,0:T(8,128)} %init_ref.1), custom_call_target="tpu_custom_call" | custom-call | tf_op jit(solution)/shard_map/fast_weight_step/pallas_call | solution.py:264
  132.0 3.2 %copy.10 = bf16[512,2048]{1,0:T(8,128)(2,1)} copy(bf16[512,2048]{1,0:T(8,128)(2,1)} %fast_weight_step.1) | data formatting | bytes 4194304

commit v2 on v1

--- a/solution.py
+++ b/solution.py
@@ -24,7 +24,7 @@
 def step_kernel(
     dims,
     q_hbm, k_hbm, v_hbm, rates_ref, split_ref, init_ref, out_ref,
-    q_ref, k_ref, v_ref, w, grad, half, core_in, quarter, y_in, z_in, state, momentum,
+    q_ref, k_ref, v_ref, w, own, grad, half, core_in, quarter, y_in, z_in, state, momentum,
     load_sem, agz_s, agz_r, agy_s, agy_r, agc_s, agc_r,
     rsc_s, rsc_r, rsy_s, rsy_r, rsz_s, rsz_r,
 ):
@@ -60,22 +60,23 @@
             for i, zp in enumerate(z_peers)
         ]
 
-    def ag_y_copy(r, h):
-        mine = w.at[r, h, :, y0, c0]
-        return remote(mine, mine, agy_s.at[r, h], agy_r.at[r, h], y_peer)
-
-    def ag_c_copy(r, h):
-        mine = w.at[r, h, :, :, c0]
-        return remote(mine, mine, agc_s.at[r, h], agc_r.at[r, h], partner)
-
-    def rs_c_copy(r, h):
+    def ag_y_copy(r, h, z):
+        mine = w.at[r, h, z, y0, c0]
+        return remote(mine, mine, agy_s.at[r, h, z], agy_r.at[r, h, z], y_peer)
+
+    def ag_c_copy(r, h, y):
+        mine = w.at[r, h, :, y, c0]
+        return remote(mine, mine, agc_s.at[r, h, y], agc_r.at[r, h, y], partner)
+
+    def rs_c_copy(r, h, y):
         return remote(
-            grad.at[r, h, :, :, c1], core_in.at[r, h], rsc_s.at[r, h], rsc_r.at[r, h], partner
+            grad.at[r, h, :, y, c1], core_in.at[r, h, :, y],
+            rsc_s.at[r, h, y], rsc_r.at[r, h, y], partner,
         )
 
-    def rs_y_copy(r, h):
+    def rs_y_copy(r, h, z):
         return remote(
-            half.at[r, h, :, y1], y_in.at[r, h], rsy_s.at[r, h], rsy_r.at[r, h], y_peer
+            half.at[r, h, z], y_in.at[r, h, z], rsy_s.at[r, h, z], rsy_r.at[r, h, z], y_peer
         )
 
     def rs_z_copies(r, h):
@@ -90,17 +91,25 @@
     def ag_z(r, h):
         for copy in ag_z_copies(r, h):
             copy.start()
+        ag_y_copy(r, h, z0).start()
 
     def ag_y(r, h):
         for i, zp in enumerate(z_peers):
             there = w.at[r, h, zp, y0, c0]
             remote(there, there, agz_s.at[r, h, i], agz_r.at[r, h, zp], y_peer).wait_recv()
-        ag_y_copy(r, h).start()
+            ag_y_copy(r, h, zp).start()
+        ag_c_copy(r, h, y0).start()
 
     def ag_c(r, h):
-        there = w.at[r, h, :, y1, c0]
-        remote(there, there, agy_s.at[r, h], agy_r.at[r, h], y_peer).wait_recv()
-        ag_c_copy(r, h).start()
+        for z in range(nz):
+            there = w.at[r, h, z, y1, c0]
+            remote(there, there, agy_s.at[r, h, z], agy_r.at[r, h, z], y_peer).wait_recv()
+        ag_c_copy(r, h, y1).start()
+
+    def ag_wait(r, h):
+        for y in range(NY):
+            there = w.at[r, h, :, y, c1]
+            remote(there, there, agc_s.at[r, h, y], agc_r.at[r, h, y], partner).wait_recv()
 
     def gathered(r, h):
         return w[r, h].reshape(width, 3 * hidden)
@@ -109,8 +118,7 @@
         return pl.ds(pl.multiple_of(h * width, width), width)
 
     def gradient(r, h):
-        there = w.at[r, h, :, :, c1]
-        remote(there, there, agc_s.at[r, h], agc_r.at[r, h], partner).wait_recv()
+        ag_wait(r, h)
         low = 0 if r == 0 else rows - trimmed
         weights = gathered(r, h)
         keys = k_ref[low : low + trimmed, head_columns(h)]
@@ -118,9 +126,10 @@
         row = low + lax.broadcasted_iota(jnp.int32, (trimmed, 1), 0)
         first = row < split_ref[0]
         keep = first if r == 0 else jnp.logical_not(first)
-        all_rates = rates_ref[low : low + trimmed, :]
-        lane = lax.broadcasted_iota(jnp.int32, all_rates.shape, 1)
-        rate = jnp.sum(jnp.where(lane == h, all_rates, 0.0), axis=1, keepdims=True)
+        across = lax.broadcasted_iota(jnp.int32, (trimmed, trimmed), 0)
+        along = lax.broadcasted_iota(jnp.int32, (trimmed, trimmed), 1)
+        rate_row = rates_ref[pl.ds(h, 1), low : low + trimmed]
+        rate = jnp.sum(jnp.where(across == along, rate_row, 0.0), axis=1, keepdims=True)
         scale = -(rate * keep.astype(F32))
         dout = (scale * values.astype(F32)).astype(BF16)
         both = dot(keys, weights[:, : 2 * hidden], 1, 0)
@@ -133,30 +142,36 @@
         du = (dhid * active).astype(BF16)
         to_both = dot(keys, jnp.concatenate([dg, du], axis=1), 0, 0)
         to_down = dot(dout, hid, 0, 0)
-        grad[r, h, :, :, :, :, : 2 * hidden] = to_both.astype(BF16).reshape(
-            nz, NY, NC, owned, 2 * hidden
-        )
-        grad[r, h, :, :, :, :, 2 * hidden :] = to_down.astype(BF16).reshape(
-            nz, NY, NC, owned, hidden
-        )
-        rs_c_copy(r, h).start()
+        to_both = to_both.reshape(nz, NY, NC, owned, 2 * hidden)
+        to_down = to_down.reshape(nz, NY, NC, owned, hidden)
+        grad[r, h, :, :, :, :, : 2 * hidden] = to_both.astype(BF16)
+        grad[r, h, :, :, :, :, 2 * hidden :] = to_down.astype(BF16)
+        rs_c_copy(r, h, y1).start()
+        rs_c_copy(r, h, y0).start()
+        own[h, :, :, :, :, : 2 * hidden] = to_both
+        own[h, :, :, :, :, 2 * hidden :] = to_down
 
     def rs_y(r, h):
-        rs_c_copy(r, h).wait_recv()
-        half[r, h] = (grad[r, h, :, :, c0].astype(F32) + core_in[r, h].astype(F32)).astype(BF16)
-        rs_y_copy(r, h).start()
+        rs_c_copy(r, h, y1).wait_recv()
+        for z in z_peers + [z0]:
+            half[r, h, z] = (own[h, z, y1, c0] + core_in[r, h, z, y1].astype(F32)).astype(BF16)
+            rs_y_copy(r, h, z).start()
+
+    def pair_sum(r, h, z):
+        rs_y_copy(r, h, z).wait_recv()
+        return own[h, z, y0, c0] + core_in[r, h, z, y0].astype(F32) + y_in[r, h, z].astype(F32)
 
     def rs_z(r, h):
-        rs_y_copy(r, h).wait_recv()
-        quarter[r, h] = (half[r, h, :, y0].astype(F32) + y_in[r, h].astype(F32)).astype(BF16)
-        for copy in rs_z_copies(r, h):
+        rs_c_copy(r, h, y0).wait_recv()
+        for zp, copy in zip(z_peers, rs_z_copies(r, h)):
+            quarter[r, h, zp] = pair_sum(r, h, zp).astype(BF16)
             copy.start()
 
     def initial(m, h):
         return init_ref[:, pl.ds(pl.multiple_of((m * heads + h) * hidden, hidden), hidden)]
 
     def update(r, h):
-        total = quarter[r, h, z0].astype(F32)
+        total = pair_sum(r, h, z0)
         for i, zp in enumerate(z_peers):
             there = z_in.at[r, h, zp]
             remote(there, there, rsz_s.at[r, h, i], rsz_r.at[r, h, zp], y_peer).wait_recv()
@@ -191,8 +206,7 @@
         out_ref[:trimmed, head_columns(h)] = apply(1, h)
 
     def apply_second(h):
-        there = w.at[2, h, :, :, c1]
-        remote(there, there, agc_s.at[2, h], agc_r.at[2, h], partner).wait_recv()
+        ag_wait(2, h)
         second = apply(2, h)
         low = rows - trimmed
         row = low + lax.broadcasted_iota(jnp.int32, (trimmed - low, 1), 0)
@@ -240,10 +254,12 @@
 
     def drain(h, carry):
         for r in range(3):
-            for copy in ag_z_copies(r, h) + [ag_y_copy(r, h), ag_c_copy(r, h)]:
+            along_y = [ag_y_copy(r, h, z) for z in range(nz)]
+            for copy in ag_z_copies(r, h) + along_y + [ag_c_copy(r, h, y) for y in range(NY)]:
                 copy.wait_send()
         for r in range(2):
-            for copy in [rs_c_copy(r, h), rs_y_copy(r, h)] + rs_z_copies(r, h):
+            along_y = [rs_y_copy(r, h, z) for z in range(nz)]
+            for copy in rs_z_copies(r, h) + along_y + [rs_c_copy(r, h, y) for y in range(NY)]:
                 copy.wait_send()
         return carry
 
@@ -271,8 +287,9 @@
             pltpu.VMEM((rows, features), BF16),
             pltpu.VMEM((rows, features), BF16),
             pltpu.VMEM((3, heads, nz, NY, NC) + chunk, BF16),
+            pltpu.VMEM((heads, nz, NY, NC) + chunk, F32),
             pltpu.VMEM((2, heads, nz, NY, NC) + chunk, BF16),
-            pltpu.VMEM((2, heads, nz, NY) + chunk, BF16),
+            pltpu.VMEM((2, heads, nz) + chunk, BF16),
             pltpu.VMEM((2, heads, nz, NY) + chunk, BF16),
             pltpu.VMEM((2, heads, nz) + chunk, BF16),
             pltpu.VMEM((2, heads, nz) + chunk, BF16),
@@ -282,14 +299,14 @@
             dma((3,)),
             dma((3, heads, nz - 1)),
             dma((3, heads, nz)),
-            dma((3, heads)),
-            dma((3, heads)),
-            dma((3, heads)),
-            dma((3, heads)),
-            dma((2, heads)),
-            dma((2, heads)),
-            dma((2, heads)),
-            dma((2, heads)),
+            dma((3, heads, nz)),
+            dma((3, heads, nz)),
+            dma((3, heads, NY)),
+            dma((3, heads, NY)),
+            dma((2, heads, NY)),
+            dma((2, heads, NY)),
+            dma((2, heads, nz)),
+            dma((2, heads, nz)),
             dma((2, heads, nz - 1)),
             dma((2, heads, nz)),
         ],
@@ -297,7 +314,7 @@
             collective_id=0, has_side_effects=True, vmem_limit_bytes=60 * 1024 * 1024
         ),
         name="fast_weight_step",
-    )(queries, keys, values, rates, split_row, fast_init)
+    )(queries, keys, values, rates.T, split_row, fast_init)
 
 
 def gather_weights(shard, heads, hidden):

time: 135 us -> 124 us (0.919)
  Pallas kernels: 130 us -> 120 us
  local copies, waits for them, and re-layouts: 4.71 us -> 3.16 us
    pallas_call x1, Pallas kernels: 130 us -> 120 us  [fused_step(): pl.pallas_call(functools.partial(step_kernel, (heads, rows, width, hidden...]
    unnamed x2 -> x1, local copies, waits for them, and re-layouts: 4.71 us -> 3.16 us
where the time goes in v2:
time: 124 us
  Pallas kernels  120 us (97%)
  local copies, waits for them, and re-layouts  3.16 us (3%)
    pallas_call x1, Pallas kernels, fused_step(): pl.pallas_call(functools.partial(step_kernel, (heads, rows, width, hidden...  120 us
    unnamed x1, local copies, waits for them, and re-layouts  3.16 us

profile of v2, /device:TPU:1, one launch (start us, length us, event | category | flops | bytes accessed | tf_op | source)
XLA Modules:
  0.0 123.8 jit_solution(9789840983473200266)
XLA Ops:
  0.7 120.0 %fast_weight_step.1 = bf16[512,2048]{1,0:T(8,128)(2,1)} custom-call(bf16[512,2048]{1,0:T(8,128)(2,1)} %q_hbm.1, bf16[512,2048]{1,0:T(8,128)(2,1)} %k_hbm.1, bf16[512,2048]{1,0:T(8,128)(2,1)} %v_hbm.1, f32[4,512]{1,0:T(4,128)} %bitcast.1, s32[1]{0:T(128)S(6)} %copy.8.split_ref, f32[32,3072]{1,0:T(8,128)} %init_ref.1), custom_call_target="tpu_custom_call" | custom-call | tf_op jit(solution)/shard_map/fast_weight_step/pallas_call | solution.py:280
  120.7 3.2 %copy.9 = bf16[512,2048]{1,0:T(8,128)(2,1)} copy(bf16[512,2048]{1,0:T(8,128)(2,1)} %fast_weight_step.1) | data formatting | bytes 4194304

commit v3 on v2

--- a/solution.py
+++ b/solution.py
@@ -25,11 +25,12 @@
     dims,
     q_hbm, k_hbm, v_hbm, rates_ref, split_ref, init_ref, out_ref,
     q_ref, k_ref, v_ref, w, own, grad, half, core_in, quarter, y_in, z_in, state, momentum,
-    load_sem, agz_s, agz_r, agy_s, agy_r, agc_s, agc_r,
+    load_sem, agz_s, agz_r, agy_s, agy_r, agc_s, agc_r, agx_s, agx_r,
     rsc_s, rsc_r, rsy_s, rsy_r, rsz_s, rsz_r,
 ):
     heads, rows, width, hidden, nz, owned = dims
     me = lax.axis_index("tok")
+    g0 = lax.axis_index("groups")
     c0 = lax.rem(me, NC)
     y0 = lax.rem(me // NC, NY)
     z0 = me // (NC * NY)
@@ -40,6 +41,11 @@
     def device(z, y, c):
         return {"tok": (z * NY + y) * NC + c}
 
+    x_peer = {"groups": 1 - g0}
+    gathered_here = pl.ds(pl.multiple_of(g0 * hidden, hidden), 2 * hidden)
+    sent_across = pl.ds(pl.multiple_of(g0 * 2 * hidden, hidden), hidden)
+    got_across = pl.ds(pl.multiple_of((1 - g0) * 2 * hidden, hidden), hidden)
+
     partner, y_peer = device(z0, y0, c1), device(z0, y1, c0)
 
     def remote(src, dst, send_sem, recv_sem, target):
@@ -53,15 +59,24 @@
         for i, (src, dst) in enumerate(((k_hbm, k_ref), (v_hbm, v_ref), (q_hbm, q_ref)))
     ]
 
+    def shard(r, h, z, y):
+        if r == 0:
+            return w.at[r, h, z, y, c0, :, gathered_here]
+        return w.at[r, h, z, y, c0]
+
+    def ag_x_copy(h, z, y):
+        part = w.at[0, h, z, y, c0, :, sent_across]
+        return remote(part, part, agx_s.at[h, z, y], agx_r.at[h, z, y], x_peer)
+
     def ag_z_copies(r, h):
-        mine = w.at[r, h, z0, y0, c0]
+        mine = shard(r, h, z0, y0)
         return [
             remote(mine, mine, agz_s.at[r, h, i], agz_r.at[r, h, z0], device(zp, y0, c0))
             for i, zp in enumerate(z_peers)
         ]
 
     def ag_y_copy(r, h, z):
-        mine = w.at[r, h, z, y0, c0]
+        mine = shard(r, h, z, y0)
         return remote(mine, mine, agy_s.at[r, h, z], agy_r.at[r, h, z], y_peer)
 
     def ag_c_copy(r, h, y):
@@ -94,17 +109,30 @@
         ag_y_copy(r, h, z0).start()
 
     def ag_y(r, h):
-        for i, zp in enumerate(z_peers):
-            there = w.at[r, h, zp, y0, c0]
+        for i, zp in reversed(list(enumerate(z_peers))):
+            there = shard(r, h, zp, y0)
             remote(there, there, agz_s.at[r, h, i], agz_r.at[r, h, zp], y_peer).wait_recv()
             ag_y_copy(r, h, zp).start()
-        ag_c_copy(r, h, y0).start()
+            if r == 0:
+                ag_x_copy(h, zp, y0).start()
+        if r > 0:
+            ag_c_copy(r, h, y0).start()
 
     def ag_c(r, h):
-        for z in range(nz):
-            there = w.at[r, h, z, y1, c0]
+        for z in [z0] + z_peers[::-1]:
+            there = shard(r, h, z, y1)
             remote(there, there, agy_s.at[r, h, z], agy_r.at[r, h, z], y_peer).wait_recv()
-        ag_c_copy(r, h, y1).start()
+            if r == 0:
+                ag_x_copy(h, z, y1).start()
+        if r > 0:
+            ag_c_copy(r, h, y1).start()
+
+    def ag_x(h):
+        for y, zs in ((y0, z_peers[::-1]), (y1, [z0] + z_peers[::-1])):
+            for z in zs:
+                there = w.at[0, h, z, y, c0, :, got_across]
+                remote(there, there, agx_s.at[h, z, y], agx_r.at[h, z, y], x_peer).wait_recv()
+            ag_c_copy(0, h, y).start()
 
     def ag_wait(r, h):
         for y in range(NY):
@@ -220,7 +248,7 @@
     for load in loads:
         load.start()
     barrier = pltpu.get_barrier_semaphore()
-    peers = [partner, y_peer] + [device(zp, y0, c0) for zp in z_peers]
+    peers = [partner, y_peer, x_peer] + [device(zp, y0, c0) for zp in z_peers]
     for peer in peers:
         pl.semaphore_signal(barrier, inc=1, device_id=peer, device_id_type=MESH)
     for h in range(heads):
@@ -234,11 +262,12 @@
 
     stages = []
     for r in range(2):
-        stages += [
-            functools.partial(stage, r) for stage in (ag_y, ag_c, gradient, rs_y, rs_z, update)
-        ]
+        stages += [functools.partial(ag_y, r), functools.partial(ag_c, r)]
+        if r == 0:
+            stages.append(ag_x)
+        stages += [functools.partial(stage, r) for stage in (gradient, rs_y, rs_z, update)]
     stages += [functools.partial(ag_y, 2), functools.partial(ag_c, 2), apply_second]
-    order = [(s, stages[s]) for s in reversed(range(len(stages)))] + [(9, apply_first)]
+    order = [(s, stages[s]) for s in range(len(stages))] + [(10, apply_first)]
 
     def tick(t, carry):
         for s, stage in order:
@@ -253,6 +282,9 @@
     lax.fori_loop(0, len(stages) + heads - 1, tick, 0)
 
     def drain(h, carry):
+        for y, zs in ((y0, z_peers), (y1, [z0] + z_peers)):
+            for z in zs:
+                ag_x_copy(h, z, y).wait_send()
         for r in range(3):
             along_y = [ag_y_copy(r, h, z) for z in range(nz)]
             for copy in ag_z_copies(r, h) + along_y + [ag_c_copy(r, h, y) for y in range(NY)]:
@@ -303,6 +335,8 @@
             dma((3, heads, nz)),
             dma((3, heads, NY)),
             dma((3, heads, NY)),
+            dma((heads, nz, NY)),
+            dma((heads, nz, NY)),
             dma((2, heads, NY)),
             dma((2, heads, NY)),
             dma((2, heads, nz)),
@@ -417,7 +451,7 @@
 def plan(*args):
     size = lax.axis_size("tok")
     small = size // (NY * NC) in (2, 3, 4) and size % (NY * NC) == 0
-    if small and args[5].shape[0] % 16 == 0:
+    if small and lax.axis_size("groups") == 2 and args[5].shape[0] % 16 == 0:
         return fused_step(*args)
     return per_device(*args)
 

time: 124 us -> 121 us (0.976)
  Pallas kernels: 120 us -> 117 us
    pallas_call x1, Pallas kernels: 120 us -> 117 us  [fused_step(): pl.pallas_call(functools.partial(step_kernel, (heads, rows, width, hidden...]
where the time goes in v3:
time: 121 us
  Pallas kernels  117 us (97%)
  local copies, waits for them, and re-layouts  3.16 us (3%)
    pallas_call x1, Pallas kernels, fused_step(): pl.pallas_call(functools.partial(step_kernel, (heads, rows, width, hidden...  117 us
    unnamed x1, local copies, waits for them, and re-layouts  3.16 us

profile of v3, /device:TPU:1, one launch (start us, length us, event | category | flops | bytes accessed | tf_op | source)
XLA Modules:
  0.0 121.2 jit_solution(4425346532388894783)
XLA Ops:
  0.7 117.4 %fast_weight_step.1 = bf16[512,2048]{1,0:T(8,128)(2,1)} custom-call(bf16[512,2048]{1,0:T(8,128)(2,1)} %q_hbm.1, bf16[512,2048]{1,0:T(8,128)(2,1)} %k_hbm.1, bf16[512,2048]{1,0:T(8,128)(2,1)} %v_hbm.1, f32[4,512]{1,0:T(4,128)} %bitcast.1, s32[1]{0:T(128)S(6)} %copy.8.split_ref, f32[32,3072]{1,0:T(8,128)} %init_ref.1), custom_call_target="tpu_custom_call" | custom-call | tf_op jit(solution)/shard_map/fast_weight_step/pallas_call | solution.py:312
  118.1 3.2 %copy.9 = bf16[512,2048]{1,0:T(8,128)(2,1)} copy(bf16[512,2048]{1,0:T(8,128)(2,1)} %fast_weight_step.1) | data formatting | bytes 4194304

commit v4 on v3

--- a/solution.py
+++ b/solution.py
@@ -23,9 +23,9 @@
 
 def step_kernel(
     dims,
-    q_hbm, k_hbm, v_hbm, rates_ref, split_ref, init_ref, out_ref,
-    q_ref, k_ref, v_ref, w, own, grad, half, core_in, quarter, y_in, z_in, state, momentum,
-    load_sem, agz_s, agz_r, agy_s, agy_r, agc_s, agc_r, agx_s, agx_r,
+    q_hbm, k_hbm, v_hbm, rates_ref, split_ref, init_ref, out_hbm,
+    out_ref, q_ref, k_ref, v_ref, w, own, grad, half, core_in, quarter, y_in, z_in, state, momentum,
+    load_sem, store_sem, agz_s, agz_r, agy_s, agy_r, agc_s, agc_r, agx_s, agx_r,
     rsc_s, rsc_r, rsy_s, rsy_r, rsz_s, rsz_r,
 ):
     heads, rows, width, hidden, nz, owned = dims
@@ -35,7 +35,8 @@
     y0 = lax.rem(me // NC, NY)
     z0 = me // (NC * NY)
     c1, y1 = 1 - c0, 1 - y0
-    z_peers = [lax.rem(z0 + i, nz) for i in range(1, nz)]
+    z_steps = [2, 1] + list(range(3, nz)) if nz > 3 else list(range(1, nz))
+    z_peers = [lax.rem(z0 + i, nz) for i in z_steps]
     trimmed = rows - rows // 4
 
     def device(z, y, c):
@@ -230,6 +231,12 @@
         hid = (gates * jax.nn.sigmoid(gates) * ups).astype(BF16)
         return dot(hid, weights[:, 2 * hidden :], 1, 1).astype(BF16)
 
+    def store(h):
+        columns = head_columns(h)
+        return pltpu.make_async_copy(
+            out_ref.at[:, columns], out_hbm.at[:, columns], store_sem.at[h]
+        )
+
     def apply_first(h):
         out_ref[:trimmed, head_columns(h)] = apply(1, h)
 
@@ -244,6 +251,7 @@
             second[: trimmed - low].astype(F32),
         ).astype(BF16)
         out_ref[trimmed:, head_columns(h)] = second[trimmed - low :]
+        store(h).start()
 
     for load in loads:
         load.start()
@@ -282,6 +290,7 @@
     lax.fori_loop(0, len(stages) + heads - 1, tick, 0)
 
     def drain(h, carry):
+        store(h).wait()
         for y, zs in ((y0, z_peers), (y1, [z0] + z_peers)):
             for z in zs:
                 ag_x_copy(h, z, y).wait_send()
@@ -313,8 +322,9 @@
         functools.partial(step_kernel, (heads, rows, width, hidden, nz, owned)),
         out_shape=jax.ShapeDtypeStruct((rows, features), BF16),
         in_specs=[hbm, hbm, hbm, vmem, pl.BlockSpec(memory_space=pltpu.SMEM), vmem],
-        out_specs=vmem,
+        out_specs=hbm,
         scratch_shapes=[
+            pltpu.VMEM((rows, features), BF16),
             pltpu.VMEM((rows, features), BF16),
             pltpu.VMEM((rows, features), BF16),
             pltpu.VMEM((rows, features), BF16),
@@ -329,6 +339,7 @@
             pltpu.VMEM((heads,) + chunk, F32),
             pltpu.VMEM((heads,) + chunk, F32),
             dma((3,)),
+            dma((heads,)),
             dma((3, heads, nz - 1)),
             dma((3, heads, nz)),
             dma((3, heads, nz)),

time: 121 us -> 120 us (level)
    pallas_call x1, Pallas kernels: 117 us -> 116 us  [fused_step(): pl.pallas_call(functools.partial(step_kernel, (heads, rows, width, hidden...]
where the time goes in v4:
time: 120 us
  Pallas kernels  116 us (97%)
  local copies, waits for them, and re-layouts  3.16 us (3%)
    pallas_call x1, Pallas kernels, fused_step(): pl.pallas_call(functools.partial(step_kernel, (heads, rows, width, hidden...  116 us
    unnamed x1, local copies, waits for them, and re-layouts  3.16 us

profile of v4, /device:TPU:1, one launch (start us, length us, event | category | flops | bytes accessed | tf_op | source)
XLA Modules:
  0.0 119.9 jit_solution(14558275844904420086)
XLA Ops:
  0.7 116.1 %fast_weight_step.1 = bf16[512,2048]{1,0:T(8,128)(2,1)} custom-call(bf16[512,2048]{1,0:T(8,128)(2,1)} %q_hbm.1, bf16[512,2048]{1,0:T(8,128)(2,1)} %k_hbm.1, bf16[512,2048]{1,0:T(8,128)(2,1)} %v_hbm.1, f32[4,512]{1,0:T(4,128)} %bitcast.1, s32[1]{0:T(128)S(6)} %copy.8.split_ref, f32[32,3072]{1,0:T(8,128)} %init_ref.1), custom_call_target="tpu_custom_call" | custom-call | tf_op jit(solution)/shard_map/fast_weight_step/pallas_call | solution.py:321
  116.7 3.2 %copy.9 = bf16[512,2048]{1,0:T(8,128)(2,1)} copy(bf16[512,2048]{1,0:T(8,128)(2,1)} %fast_weight_step.1) | data formatting | bytes 4194304

commit v5 on v4

--- a/solution.py
+++ b/solution.py
@@ -265,8 +265,6 @@
     pl.semaphore_wait(barrier, len(peers))
     for h in range(heads):
         ag_z(0, h)
-    for load in loads:
-        load.wait()
 
     stages = []
     for r in range(2):
@@ -278,6 +276,11 @@
     order = [(s, stages[s]) for s in range(len(stages))] + [(10, apply_first)]
 
     def tick(t, carry):
+        @pl.when(t == 2)
+        def _():
+            for load in loads:
+                load.wait()
+
         for s, stage in order:
             h = t - s
 

time: 120 us -> 120 us (level)
  no operation moved by 1% of the time
where the time goes in v5:
time: 120 us
  Pallas kernels  116 us (97%)
  local copies, waits for them, and re-layouts  3.16 us (3%)
    pallas_call x1, Pallas kernels, fused_step(): pl.pallas_call(functools.partial(step_kernel, (heads, rows, width, hidden...  116 us
    unnamed x1, local copies, waits for them, and re-layouts  3.16 us

profile of v5, /device:TPU:1, one launch (start us, length us, event | category | flops | bytes accessed | tf_op | source)
XLA Modules:
  0.0 119.9 jit_solution(16503116970150198361)
XLA Ops:
  0.7 116.1 %fast_weight_step.1 = bf16[512,2048]{1,0:T(8,128)(2,1)} custom-call(bf16[512,2048]{1,0:T(8,128)(2,1)} %q_hbm.1, bf16[512,2048]{1,0:T(8,128)(2,1)} %k_hbm.1, bf16[512,2048]{1,0:T(8,128)(2,1)} %v_hbm.1, f32[4,512]{1,0:T(4,128)} %bitcast.1, s32[1]{0:T(128)S(6)} %copy.8.split_ref, f32[32,3072]{1,0:T(8,128)} %init_ref.1), custom_call_target="tpu_custom_call" | custom-call | tf_op jit(solution)/shard_map/fast_weight_step/pallas_call | solution.py:324
  116.8 3.2 %copy.9 = bf16[512,2048]{1,0:T(8,128)(2,1)} copy(bf16[512,2048]{1,0:T(8,128)(2,1)} %fast_weight_step.1) | data formatting | bytes 4194304
